TPU v7x, 32 devices: a whole 2x2x4 slice. The times are simulated.
32 devices in a mesh: context: 8 (over z, x), channel: 4 (over y, core).
Axes of the slice: x: 2, y: 2, z: 4, core: 2. Of those that a mesh axis runs over, the one named last changes fastest.
Arguments:
- inputs: bfloat16 [2048, 2048], P('channel', 'context'), may hold values from -6 to 6
- out_grad: bfloat16 [2048, 2048], P('channel', 'context'), may hold values from -6 to 6
- low_pass: float32 [2, 2048], P(None, 'channel'), may hold values from 0.75 to 1.25
- high_pass: float32 [2, 2048], P(None, 'channel'), may hold values from -3 to 3
- level_weight: float32 [12, 2048], P(None, 'channel'), may hold values from -1.75 to 1.75
- mix: bfloat16 [2048, 2048], P(None, 'channel'), may hold values from -0.125 to 0.125
Outputs:
- grad_inputs: bfloat16 [2048, 2048], P('channel', 'context')
- grad_low: float32 [2, 2048], P(None, 'channel')
- grad_high: float32 [2, 2048], P(None, 'channel')
- grad_level: float32 [12, 2048], P(None, 'channel')
- grad_mix: float32 [2048, 2048], P('context', 'channel')
All inputs are finite; a program needn't handle non-finite values.
Results may differ from a plain program's by a relative error of at most 0.012.
Values may be sent and summed in bfloat16 or wider, within the bound.
A program may use at most 64 MiB of HBM per device.

v0:
```python
import jax
import jax.numpy as jnp
from jax import lax
from jax.sharding import PartitionSpec as P

HALF_ROOT = 0.5**0.5


def passed_along(value, axis, steps):
    count = lax.axis_size(axis)
    leading, last = (max(0, -steps), min(count, count - steps))
    return lax.ppermute(value, axis, [(source, source + steps) for source in range(leading, last)])


def advance(present, lagged, low_taps, high_taps):
    present_wide = present.astype(jnp.float32)
    lagged_wide = lagged.astype(jnp.float32)
    branch = HALF_ROOT * (high_taps[0] * present_wide + high_taps[1] * lagged_wide)
    present_next = (HALF_ROOT * (low_taps[0] * present_wide + low_taps[1] * lagged_wide)).astype(
        jnp.bfloat16
    )
    return (present_next, branch)


def terms_of(present, lagged, grad_now, grad_branch, grad_mixed, high_taps):
    present_wide = present.astype(jnp.float32)
    lagged_wide = lagged.astype(jnp.float32)
    branch = HALF_ROOT * (high_taps[0] * present_wide + high_taps[1] * lagged_wide)
    low_terms = HALF_ROOT * jnp.stack(
        [jnp.sum(present_wide * grad_now, 1), jnp.sum(lagged_wide * grad_now, 1)]
    )
    high_terms = HALF_ROOT * jnp.stack(
        [jnp.sum(present_wide * grad_branch, 1), jnp.sum(lagged_wide * grad_branch, 1)]
    )
    return (low_terms, high_terms, jnp.sum(grad_mixed * branch, 1))


def split_grad(grad_now, grad_branch, low_taps, high_taps):
    direct_part = HALF_ROOT * (low_taps[0] * grad_now + high_taps[0] * grad_branch)
    lagged_part = HALF_ROOT * (low_taps[1] * grad_now + high_taps[1] * grad_branch)
    return (direct_part, lagged_part)


def shards(inputs, out_grad, low_pass, high_pass, level_weight, mix):
    channels, length = inputs.shape
    levels = level_weight.shape[0] - 1
    local_count = length.bit_length() - 1
    low_taps = low_pass[:, :, None]
    high_taps = high_pass[:, :, None]
    weights = level_weight[:, :, None]
    stored = []
    mixed_sum = jnp.zeros((channels, length), jnp.float32)
    before = passed_along(inputs, "context", 1)
    current = jnp.concatenate([before, inputs], 1)
    for level_index in range(local_count):
        distance = 2**level_index
        pad_zeros = jnp.zeros((channels, distance), jnp.bfloat16)
        lagged = jnp.concatenate([pad_zeros, current[:, : 2 * length - distance]], 1)
        stored.append((current[:, length:], lagged[:, length:]))
        current, branch = advance(current, lagged, low_taps, high_taps)
        mixed_sum = mixed_sum + weights[level_index + 1] * branch[:, length:]
    current = current[:, length:]
    for hop_index in range(levels - local_count):
        level_index = local_count + hop_index
        lagged = passed_along(current, "context", 2**hop_index)
        stored.append((current, lagged))
        current, branch = advance(current, lagged, low_taps, high_taps)
        mixed_sum = mixed_sum + weights[level_index + 1] * branch
    mixed_sum = mixed_sum + weights[0] * current.astype(jnp.float32)
    z_out = jax.nn.gelu(mixed_sum).astype(jnp.bfloat16)
    partial_mix = lax.dot_general(
        lax.all_gather(z_out, "channel", axis=0, tiled=True),
        out_grad,
        (((1,), (1,)), ((), ())),
        preferred_element_type=jnp.float32,
    )
    scale = float(lax.axis_size("context") * length) ** (-0.5)
    grad_mix = lax.psum_scatter(partial_mix, "context", scatter_dimension=0, tiled=True) * scale
    grad_z = lax.psum_scatter(
        jnp.dot(mix, out_grad, preferred_element_type=jnp.float32),
        "channel",
        scatter_dimension=0,
        tiled=True,
    )
    grad_mixed = jax.vjp(jax.nn.gelu, mixed_sum)[1](grad_z)[0]
    totals = [jnp.zeros((2, channels), jnp.float32), jnp.zeros((2, channels), jnp.float32)]
    rows_out = [None] * (levels + 1)
    first_row = jnp.sum(grad_mixed * current.astype(jnp.float32), 1)

    def record(level_index, found):
        found = lax.psum(found, "context")
        totals[0] = totals[0] + found[0]
        totals[1] = totals[1] + found[1]
        rows_out[level_index + 1] = found[2]
        if len(found) == 4:
            rows_out[0] = found[3]

    grad_now = weights[0] * grad_mixed
    for step_index in range(levels - local_count):
        level_index = levels - 1 - step_index
        hop_index = level_index - local_count
        present, lagged = stored[level_index]
        grad_branch = weights[level_index + 1] * grad_mixed
        found = terms_of(present, lagged, grad_now, grad_branch, grad_mixed, high_taps)
        if step_index == 0:
            found = found + (first_row,)
        record(level_index, found)
        direct_part, lagged_part = split_grad(grad_now, grad_branch, low_taps, high_taps)
        grad_now = direct_part + passed_along(lagged_part, "context", -(2**hop_index))
    after = passed_along((grad_now, grad_mixed), "context", -1)
    grad_window = jnp.concatenate([grad_now, after[0]], 1)
    mixed_window = jnp.concatenate([grad_mixed, after[1]], 1)
    for step_index in range(local_count):
        level_index = local_count - 1 - step_index
        distance = 2**level_index
        present, lagged = stored[level_index]
        grad_branch = weights[level_index + 1] * mixed_window
        record(
            level_index,
            terms_of(
                present,
                lagged,
                grad_window[:, :length],
                grad_branch[:, :length],
                grad_mixed,
                high_taps,
            ),
        )
        direct_part, lagged_part = split_grad(grad_window, grad_branch, low_taps, high_taps)
        pad_zeros = jnp.zeros((channels, distance), jnp.float32)
        grad_window = direct_part + jnp.concatenate([lagged_part[:, distance:], pad_zeros], 1)
    grad_now = grad_window[:, :length]
    low_grad, high_grad, level_grad = (totals[0], totals[1], jnp.stack(rows_out))
    return (
        grad_now.astype(jnp.bfloat16),
        low_grad * scale,
        high_grad * scale,
        level_grad * scale,
        grad_mix,
    )


def solution(mesh):
    return jax.shard_map(
        shards,
        mesh=mesh,
        in_specs=(
            P("channel", "context"),
            P("channel", "context"),
            P(None, "channel"),
            P(None, "channel"),
            P(None, "channel"),
            P(None, "channel"),
        ),
        out_specs=(
            P("channel", "context"),
            P(None, "channel"),
            P(None, "channel"),
            P(None, "channel"),
            P("context", "channel"),
        ),
        check_vma=False,
    )
```

profile of v0, /device:TPU:0, one launch (start us, length us, event | category | flops | bytes accessed | tf_op | source)
XLA Modules:
  0.0 235.0 jit_solution(10075581194291830339)
XLA Ops:
  7.2 5.0 %collective-permute-start = (bf16[512,256]{1,0:T(8,128)(2,1)}, bf16[512,256]{1,0:T(8,128)(2,1)S(1)}, u32[]{:S(2)}, u32[]{:S(2)}) collective-permute-start(bf16[512,256]{1,0:T(8,128)(2,1)} %param.6), channel_id=1, source_target_pairs={{0,4},{4,8},{8,12},{12,16},{16,20},{20,24},{24,28},{1,5},{5,9},{9,... | collective-permute-start | bytes 786440 | tf_op jit(solution)/shard_map/ppermute | solution.py:12
  12.3 3.0 %fusion.180 = f32[2048,256]{1,0:T(8,128)} fusion(bf16[2048,512]{1,0:T(8,128)(2,1)S(1)} %copy-done, bf16[512,256]{1,0:T(8,128)(2,1)} %param.7), kind=kOutput, calls=%fused_computation.341 | convolution fusion | flops 536870912 | bytes 4456448 | tf_op jit(solution)/shard_map/dot_general | solution.py:80
  15.4 0.6 copy-done.28
  16.1 2.0 collective-permute-done
  18.2 0.6 fusion.171
  18.8 0.6 fusion.172
  19.4 0.6 fusion.173
  20.0 0.6 fusion.174
  20.6 0.6 fusion.175
  21.2 0.6 fusion.176
  21.9 0.6 fusion.170
  22.9 4.3 %collective-permute-start.1 = (bf16[512,256]{1,0:T(8,128)(2,1)S(1)}, bf16[512,256]{1,0:T(8,128)(2,1)S(1)}, u32[]{:S(2)}, u32[]{:S(2)}) collective-permute-start(bf16[512,256]{1,0:T(8,128)(2,1)S(1)} %multiply_convert_fusion.8), channel_id=1, source_target_pairs={{0,4},{4,8},{8,12},{12,16},{16,20},{20,24},{24,28},{1,5},{5,9},{9,... | collective-permute-start | bytes 786440 | tf_op jit(solution)/shard_map/ppermute | solution.py:12
  27.3 4.5 %collective-permute-done.1 = bf16[512,256]{1,0:T(8,128)(2,1)S(1)} collective-permute-done((bf16[512,256]{1,0:T(8,128)(2,1)S(1)}, bf16[512,256]{1,0:T(8,128)(2,1)S(1)}, u32[]{:S(2)}, u32[]{:S(2)}) %collective-permute-start.1) | collective-permute-done | bytes 262176 | tf_op jit(solution)/shard_map/ppermute | solution.py:12
  32.1 6.3 %collective-permute-start.2 = (bf16[512,256]{1,0:T(8,128)(2,1)S(1)}, bf16[512,256]{1,0:T(8,128)(2,1)S(1)}, u32[]{:S(2)}, u32[]{:S(2)}) collective-permute-start(bf16[512,256]{1,0:T(8,128)(2,1)S(1)} %fusion.97), channel_id=1, source_target_pairs={{0,8},{4,12},{8,16},{12,20},{16,24},{20,28},{1,9},{5,13},{9,17},{1... | collective-permute-start | bytes 786440 | tf_op jit(solution)/shard_map/ppermute | solution.py:12
  38.4 0.5 pad_convert_fusion.1
  38.9 0.5 pad_convert_fusion.3
  39.3 2.9 %collective-permute-done.2 = bf16[512,256]{1,0:T(8,128)(2,1)S(1)} collective-permute-done((bf16[512,256]{1,0:T(8,128)(2,1)S(1)}, bf16[512,256]{1,0:T(8,128)(2,1)S(1)}, u32[]{:S(2)}, u32[]{:S(2)}) %collective-permute-start.2) | collective-permute-done | bytes 262176 | tf_op jit(solution)/shard_map/ppermute | solution.py:12
  42.4 5.4 %collective-permute-start.3 = (bf16[512,256]{1,0:T(8,128)(2,1)S(1)}, bf16[512,256]{1,0:T(8,128)(2,1)S(1)}, u32[]{:S(2)}, u32[]{:S(2)}) collective-permute-start(bf16[512,256]{1,0:T(8,128)(2,1)S(1)} %fusion.105), channel_id=1, source_target_pairs={{0,16},{4,20},{8,24},{12,28},{1,17},{5,21},{9,25},{13,29},{2,18},{... | collective-permute-start | bytes 786440 | tf_op jit(solution)/shard_map/ppermute | solution.py:12
  48.2 0.5 pad_convert_fusion.5
  48.7 3.1 %collective-permute-done.3 = bf16[512,256]{1,0:T(8,128)(2,1)S(1)} collective-permute-done((bf16[512,256]{1,0:T(8,128)(2,1)S(1)}, bf16[512,256]{1,0:T(8,128)(2,1)S(1)}, u32[]{:S(2)}, u32[]{:S(2)}) %collective-permute-start.3) | collective-permute-done | bytes 262176 | tf_op jit(solution)/shard_map/ppermute | solution.py:12
  51.8 2.8 %multiply_convert_fusion.7 = (bf16[512,256]{1,0:T(8,128)(2,1)}, f32[512,256]{1,0:T(8,128)}) fusion(f32[512]{0:T(512)S(1)} %bitcast.107, f32[512]{0:T(512)S(1)} %bitcast.130, f32[512]{0:T(512)S(1)} %bitcast.183, f32[512]{0:T(512)S(1)} %get-tuple-element.151, bf16[512,256]{1,0:T(8,128)(2,1)S(1)} %collective-permute-done.3, bf16[512,256]{1,0:T(8,128)(2,1)S(1)} %fusion.105, ...), kind=kLoop, calls=%fused_computation.273 | loop fusion | flops 11141120 | bytes 10780672 | tf_op jit(solution)/shard_map/convert_element_type | solution.py:70
  54.7 4.7 %multiply_reduce_fusion.1 = (f32[512]{0:T(512)S(1)}, f32[512]{0:T(512)S(1)}, f32[512]{0:T(512)S(1)}, f32[512]{0:T(512)S(1)}, f32[512]{0:T(512)S(1)}, /*index=5*/...) fusion(bf16[512,256]{1,0:T(8,128)(2,1)} %copy-done.19, ...), kind=kLoop, calls=%fused_computation.275 | loop fusion | flops 11135488 | bytes 5273600 | tf_op jit(solution)/shard_map/reduce_sum | solution.py:35
  59.4 0.3 add_multiply_fusion.2
  59.8 1.3 collective-permute-start.4
  61.1 23.1 %collective-permute-done.4 = f32[512,256]{1,0:T(8,128)S(1)} collective-permute-done((f32[512,256]{1,0:T(8,128)S(1)}, f32[512,256]{1,0:T(8,128)S(1)}, u32[]{:S(2)}, u32[]{:S(2)}) %collective-permute-start.4) | collective-permute-done | bytes 524320 | tf_op jit(solution)/shard_map/ppermute | solution.py:12
  84.1 0.5 fusion.106
  84.6 0.8 copy-done.17
  85.5 1.1 add_multiply_fusion.1
  86.6 1.3 collective-permute-start.5
  87.9 3.9 %fusion.181 = f32[2048,512]{1,0:T(8,128)} fusion(bf16[2048,256]{1,0:T(8,128)(2,1)} %all-gather.2.cloned.1.call-done, bf16[512,256]{1,0:T(8,128)(2,1)} %param.7), kind=kOutput, calls=%fused_computation.342 | convolution fusion | flops 536870912 | bytes 5505024 | tf_op jit(solution)/shard_map/dot_general | solution.py:71
  91.8 1.3 collective-permute-start.8
  93.1 16.2 %collective-permute-done.5 = f32[512,256]{1,0:T(8,128)} collective-permute-done((f32[512,256]{1,0:T(8,128)}, f32[512,256]{1,0:T(8,128)}, u32[]{:S(2)}, u32[]{:S(2)}) %collective-permute-start.5) | collective-permute-done | bytes 524320 | tf_op jit(solution)/shard_map/ppermute | solution.py:12
  109.3 1.7 fusion.98
  111.3 1.4 collective-permute-start.6
  112.8 0.6 collective-permute-done.8
  113.3 0.5 broadcast_multiply_fusion.7
  113.8 13.0 %collective-permute-done.6 = f32[512,256]{1,0:T(8,128)S(1)} collective-permute-done((f32[512,256]{1,0:T(8,128)S(1)}, f32[512,256]{1,0:T(8,128)S(1)}, u32[]{:S(2)}, u32[]{:S(2)}) %collective-permute-start.6) | collective-permute-done | bytes 524320 | tf_op jit(solution)/shard_map/ppermute | solution.py:12
  126.8 0.7 fusion.31
  127.5 1.5 collective-permute-start.7
  129.2 42.9 %collective-permute-done.7 = f32[512,256]{1,0:T(8,128)S(1)} collective-permute-done((f32[512,256]{1,0:T(8,128)S(1)}, f32[512,256]{1,0:T(8,128)S(1)}, u32[]{:S(2)}, u32[]{:S(2)}) %collective-permute-start.7) | collective-permute-done | bytes 524320 | tf_op jit(solution)/shard_map/ppermute | solution.py:12
  172.5 0.8 copy-done.8
  173.3 0.7 fusion.39
  173.9 0.8 fusion.17
  175.0 0.7 copy-done.6
  175.7 0.7 fusion.47
  176.4 0.8 fusion.15
  177.5 0.7 copy-done.4
  178.2 0.7 fusion.55
  178.9 0.8 fusion.13
  179.9 0.7 copy-done.2
  180.7 0.7 fusion.63
  181.3 0.8 fusion.11
  182.4 0.7 fusion.71
  183.0 0.8 fusion.9
  184.1 0.8 copy-done.12
  184.8 0.8 fusion.79
  185.6 0.7 fusion.7
  186.7 0.7 fusion.5
  187.9 2.5 %fusion.86 = (f32[512]{0:T(512)S(1)}, f32[512]{0:T(512)S(1)}, f32[512]{0:T(512)S(1)}, f32[512]{0:T(512)S(1)}, f32[512]{0:T(512)S(1)}, /*index=5*/f32[512]{0:T(51...) fusion(bf16[512,256]{1,0:T(8,128)(2,1)S(1)} %copy-done.24, ...), kind=kLoop, calls=%fused_computation.194 | loop fusion | flops 7333888 | bytes 4491264 | tf_op jit(solution)/shard_map/reduce_sum | solution.py:30
  190.5 34.1 %all-reduce.16 = (f32[2,512]{1,0:T(2,128)S(1)}, f32[2,512]{1,0:T(2,128)S(1)}, f32[1,512]{1,0:T(1,128)S(1)}, f32[1,512]{1,0:T(1,128)S(1)}, f32[1,512]{1,0:T(1,128...) all-reduce(f32[2,512]{1,0:T(2,128)S(1)} %fusion.167, ...), channel_id=1, replica_groups=mesh['context'=8,'channel'=4] {'context'}, use_global_device_ids=true, to_apply=%region_3.0 | all-reduce | flops 8192 | bytes 65536 | tf_op jit(solution)/shard_map/psum | solution.py:91
  224.7 0.6 broadcast_multiply_fusion.10
  225.3 0.6 broadcast_multiply_fusion.11
  225.9 0.6 broadcast_multiply_fusion.9
  226.5 1.9 broadcast_multiply_fusion.8
  (89 shorter events, 5.0 us)
Async XLA Ops:
  7.2 5.1 %copy-start = (bf16[2048,512]{1,0:T(8,128)(2,1)S(1)}, bf16[2048,512]{1,0:T(8,128)(2,1)}, u32[]{:S(2)}) copy-start(bf16[2048,512]{1,0:T(8,128)(2,1)} %param.11) | copy-start | bytes 6291460
  7.2 47.5 %reduce-scatter.3.cloned.1.call-start = ((), (), s32[]{:S(2)}) async-start(), calls=%async_computation.2 | async-start | bytes 2621440 | tf_op jit(solution)/shard_map/reduce_scatter | solution.py:79
  7.2 10.9 %collective-permute-start = (bf16[512,256]{1,0:T(8,128)(2,1)}, bf16[512,256]{1,0:T(8,128)(2,1)S(1)}, u32[]{:S(2)}, u32[]{:S(2)}) collective-permute-start(bf16[512,256]{1,0:T(8,128)(2,1)} %param.6), channel_id=1, source_target_pairs={{0,4},{4,8},{8,12},{12,16},{16,20},{20,24},{24,28},{1,5},{5,9},{9,... | collective-permute-start | bytes 786440 | tf_op jit(solution)/shard_map/ppermute | solution.py:12
  15.3 0.7 copy-start.28
  15.3 0.7 copy-start.29
  15.3 0.8 copy-start.27
  15.3 2.8 %copy-start.23 = (bf16[512,256]{1,0:T(8,128)(2,1)S(1)}, bf16[512,256]{1,0:T(8,128)(2,1)}, u32[]{:S(2)}) copy-start(bf16[512,256]{1,0:T(8,128)(2,1)} %param.6) | copy-start | bytes 786436
  15.3 72.6 %all-gather.2.cloned.1.call-start = ((), (), s32[]{:S(2)}) async-start(), calls=%async_computation.3 | async-start | bytes 1310720 | tf_op jit(solution)/shard_map/all_gather | solution.py:72
  18.2 29.7 %copy-start.9 = (bf16[512,512]{1,0:T(8,128)(2,1)}, bf16[512,512]{1,0:T(8,128)(2,1)S(1)}, u32[]{:S(2)}) copy-start(bf16[512,512]{1,0:T(8,128)(2,1)S(1)} %constant_dynamic-update-slice_fusion) | copy-start | bytes 1572868
  18.8 29.4 %copy-start.11 = (bf16[512,512]{1,0:T(8,128)(2,1)}, bf16[512,512]{1,0:T(8,128)(2,1)S(1)}, u32[]{:S(2)}) copy-start(bf16[512,512]{1,0:T(8,128)(2,1)S(1)} %get-tuple-element.109) | copy-start | bytes 1572868
  20.0 18.9 %copy-start.1 = (bf16[512,512]{1,0:T(8,128)(2,1)}, bf16[512,512]{1,0:T(8,128)(2,1)S(1)}, u32[]{:S(2)}) copy-start(bf16[512,512]{1,0:T(8,128)(2,1)S(1)} %get-tuple-element.113) | copy-start | bytes 1572868
  20.6 18.3 %copy-start.3 = (bf16[512,512]{1,0:T(8,128)(2,1)}, bf16[512,512]{1,0:T(8,128)(2,1)S(1)}, u32[]{:S(2)}) copy-start(bf16[512,512]{1,0:T(8,128)(2,1)S(1)} %get-tuple-element.115) | copy-start | bytes 1572868
  21.2 17.1 %copy-start.5 = (bf16[512,512]{1,0:T(8,128)(2,1)}, bf16[512,512]{1,0:T(8,128)(2,1)S(1)}, u32[]{:S(2)}) copy-start(bf16[512,512]{1,0:T(8,128)(2,1)S(1)} %get-tuple-element.117) | copy-start | bytes 1572868
  21.8 16.5 %copy-start.7 = (bf16[512,512]{1,0:T(8,128)(2,1)}, bf16[512,512]{1,0:T(8,128)(2,1)S(1)}, u32[]{:S(2)}) copy-start(bf16[512,512]{1,0:T(8,128)(2,1)S(1)} %get-tuple-element.119) | copy-start | bytes 1572868
  22.5 4.9 %copy-start.13 = (bf16[512,512]{1,0:T(8,128)(2,1)}, bf16[512,512]{1,0:T(8,128)(2,1)S(1)}, u32[]{:S(2)}) copy-start(bf16[512,512]{1,0:T(8,128)(2,1)S(1)} %get-tuple-element.107) | copy-start | bytes 1572868
  22.9 9.0 %collective-permute-start.1 = (bf16[512,256]{1,0:T(8,128)(2,1)S(1)}, bf16[512,256]{1,0:T(8,128)(2,1)S(1)}, u32[]{:S(2)}, u32[]{:S(2)}) collective-permute-start(bf16[512,256]{1,0:T(8,128)(2,1)S(1)} %multiply_convert_fusion.8), channel_id=1, source_target_pairs={{0,4},{4,8},{8,12},{12,16},{16,20},{20,24},{24,28},{1,5},{5,9},{9,... | collective-permute-start | bytes 786440 | tf_op jit(solution)/shard_map/ppermute | solution.py:12
  31.8 19.9 %copy-start.18 = (bf16[512,256]{1,0:T(8,128)(2,1)}, bf16[512,256]{1,0:T(8,128)(2,1)S(1)}, u32[]{:S(2)}) copy-start(bf16[512,256]{1,0:T(8,128)(2,1)S(1)} %collective-permute-done.1) | copy-start | bytes 786436
  32.1 19.7 %copy-start.15 = (bf16[512,256]{1,0:T(8,128)(2,1)}, bf16[512,256]{1,0:T(8,128)(2,1)S(1)}, u32[]{:S(2)}) copy-start(bf16[512,256]{1,0:T(8,128)(2,1)S(1)} %fusion.97) | copy-start | bytes 786436
  32.1 10.1 %collective-permute-start.2 = (bf16[512,256]{1,0:T(8,128)(2,1)S(1)}, bf16[512,256]{1,0:T(8,128)(2,1)S(1)}, u32[]{:S(2)}, u32[]{:S(2)}) collective-permute-start(bf16[512,256]{1,0:T(8,128)(2,1)S(1)} %fusion.97), channel_id=1, source_target_pairs={{0,8},{4,12},{8,16},{12,20},{16,24},{20,28},{1,9},{5,13},{9,17},{1... | collective-permute-start | bytes 786440 | tf_op jit(solution)/shard_map/ppermute | solution.py:12
  42.2 9.6 %copy-start.19 = (bf16[512,256]{1,0:T(8,128)(2,1)}, bf16[512,256]{1,0:T(8,128)(2,1)S(1)}, u32[]{:S(2)}) copy-start(bf16[512,256]{1,0:T(8,128)(2,1)S(1)} %collective-permute-done.2) | copy-start | bytes 786436
  42.4 9.4 %copy-start.21 = (bf16[512,256]{1,0:T(8,128)(2,1)}, bf16[512,256]{1,0:T(8,128)(2,1)S(1)}, u32[]{:S(2)}) copy-start(bf16[512,256]{1,0:T(8,128)(2,1)S(1)} %fusion.105) | copy-start | bytes 786436
  42.4 9.3 %collective-permute-start.3 = (bf16[512,256]{1,0:T(8,128)(2,1)S(1)}, bf16[512,256]{1,0:T(8,128)(2,1)S(1)}, u32[]{:S(2)}, u32[]{:S(2)}) collective-permute-start(bf16[512,256]{1,0:T(8,128)(2,1)S(1)} %fusion.105), channel_id=1, source_target_pairs={{0,16},{4,20},{8,24},{12,28},{1,17},{5,21},{9,25},{13,29},{2,18},{... | collective-permute-start | bytes 786440 | tf_op jit(solution)/shard_map/ppermute | solution.py:12
  51.8 2.9 %copy-start.25 = (bf16[512,256]{1,0:T(8,128)(2,1)}, bf16[512,256]{1,0:T(8,128)(2,1)S(1)}, u32[]{:S(2)}) copy-start(bf16[512,256]{1,0:T(8,128)(2,1)S(1)} %collective-permute-done.3) | copy-start | bytes 786436
  54.6 171.9 %reduce-scatter.5.cloned.1.call-start = ((), (), s32[]{:S(2)}) async-start(), calls=%async_computation.4 | async-start | bytes 4718592 | tf_op jit(solution)/shard_map/reduce_scatter | solution.py:78
  54.7 29.4 %copy-start.16 = (bf16[512,256]{1,0:T(8,128)(2,1)S(1)}, bf16[512,256]{1,0:T(8,128)(2,1)}, u32[]{:S(2)}) copy-start(bf16[512,256]{1,0:T(8,128)(2,1)} %copy-done.15) | copy-start | bytes 786436
  54.7 29.4 %copy-start.20 = (bf16[512,256]{1,0:T(8,128)(2,1)S(1)}, bf16[512,256]{1,0:T(8,128)(2,1)}, u32[]{:S(2)}) copy-start(bf16[512,256]{1,0:T(8,128)(2,1)} %copy-done.19) | copy-start | bytes 786436
  59.8 24.4 %collective-permute-start.4 = (f32[512,256]{1,0:T(8,128)S(1)}, f32[512,256]{1,0:T(8,128)S(1)}, u32[]{:S(2)}, u32[]{:S(2)}) collective-permute-start(f32[512,256]{1,0:T(8,128)S(1)} %add_multiply_fusion.2), channel_id=1, source_target_pairs={{16,0},{20,4},{24,8},{28,12},{17,1},{21,5},{25,9},{29,13},{18,2},{... | collective-permute-start | bytes 1572872 | tf_op jit(solution)/shard_map/ppermute | solution.py:12
  84.6 0.9 copy-start.17
  86.6 22.8 %collective-permute-start.5 = (f32[512,256]{1,0:T(8,128)}, f32[512,256]{1,0:T(8,128)}, u32[]{:S(2)}, u32[]{:S(2)}) collective-permute-start(f32[512,256]{1,0:T(8,128)} %add_multiply_fusion.1), channel_id=1, source_target_pairs={{8,0},{12,4},{16,8},{20,12},{24,16},{28,20},{9,1},{13,5},{17,9},{2... | collective-permute-start | bytes 1572872 | tf_op jit(solution)/shard_map/ppermute | solution.py:12
  91.8 21.5 %collective-permute-start.8 = (f32[512,256]{1,0:T(8,128)S(1)}, f32[512,256]{1,0:T(8,128)S(1)}, u32[]{:S(2)}, u32[]{:S(2)}) collective-permute-start(f32[512,256]{1,0:T(8,128)S(1)} %get-tuple-element.102), channel_id=1, source_target_pairs={{4,0},{8,4},{12,8},{16,12},{20,16},{24,20},{28,24},{5,1},{9,5},{13... | collective-permute-start | bytes 1572872 | tf_op jit(solution)/shard_map/ppermute | solution.py:12
  111.3 15.5 %copy-start.14 = (bf16[512,512]{1,0:T(8,128)(2,1)S(1)}, bf16[512,512]{1,0:T(8,128)(2,1)}, u32[]{:S(2)}) copy-start(bf16[512,512]{1,0:T(8,128)(2,1)} %copy-done.13) | copy-start | bytes 1572868
  111.3 15.4 %collective-permute-start.6 = (f32[512,256]{1,0:T(8,128)S(1)}, f32[512,256]{1,0:T(8,128)S(1)}, u32[]{:S(2)}, u32[]{:S(2)}) collective-permute-start(f32[512,256]{1,0:T(8,128)S(1)} %add_multiply_fusion), channel_id=1, source_target_pairs={{4,0},{8,4},{12,8},{16,12},{20,16},{24,20},{28,24},{5,1},{9,5},{13... | collective-permute-start | bytes 1572872 | tf_op jit(solution)/shard_map/ppermute | solution.py:12
  127.5 44.5 %collective-permute-start.7 = (f32[512,256]{1,0:T(8,128)S(1)}, f32[512,256]{1,0:T(8,128)S(1)}, u32[]{:S(2)}, u32[]{:S(2)}) collective-permute-start(f32[512,256]{1,0:T(8,128)S(1)} %get-tuple-element.105), channel_id=1, source_target_pairs={{4,0},{8,4},{12,8},{16,12},{20,16},{24,20},{28,24},{5,1},{9,5},{13... | collective-permute-start | bytes 1572872 | tf_op jit(solution)/shard_map/ppermute | solution.py:12
  172.2 1.0 copy-start.8
  174.7 1.0 copy-start.6
  177.2 1.0 copy-start.4
  179.6 1.0 copy-start.2
  183.8 1.0 copy-start.12
  186.6 1.0 copy-start.10
  186.6 1.1 copy-start.22
  186.7 1.2 copy-start.24
  186.7 1.2 copy-start.26
Sparse Core Ops, SparseCore 0:
  15.4 31.4 reduce-scatter.2
  54.8 22.4 all-gather.1
  92.0 116.9 reduce-scatter.4
where the time goes:
time: 236 us; the launch traced here: 235 us
  waiting for transfers between devices  108 us (46%)
  other arithmetic  37.4 us (16%)
  blocking collectives  34.1 us (14%)
  starting transfers between devices  27.9 us (12%)
  between operations  14.4 us (6%)
  matrix products  6.95 us (3%)
  local copies, waits for them, and re-layouts  5.99 us (3%)
    ppermute x9, waiting for transfers between devices, passed_along(): lax.ppermute(value, axis, [(source, source + steps) for source in range(l...  108 us
    psum x1, blocking collectives, record(): found = lax.psum(found, 'context')  34.1 us
    ppermute x9, starting transfers between devices, passed_along(): lax.ppermute(value, axis, [(source, source + steps) for source in range(l...  27.8 us
    mul x11, other arithmetic, split_grad(): HALF_ROOT * (low_taps[1] * grad_now + high_taps[1] * grad_branch)  7.13 us
    unnamed x61, local copies, waits for them, and re-layouts  5.84 us
    reduce_sum x7, other arithmetic, terms_of(): jnp.sum(present_wide * grad_branch, 1)  4.82 us
    reduce_sum x3, other arithmetic, terms_of(): jnp.sum(present_wide * grad_now, 1)  4.75 us
  transfers between devices with their start and end apart: 12, of which 9 were waited for; matrix products, arithmetic and copies ran while one was open for 18% of the time, Pallas kernels for 0%

commit v1 on v0

v1 whole, which is shorter than its diff:
```python
import functools

import jax
import jax.numpy as jnp
from jax import lax
from jax.experimental import pallas as pl
from jax.experimental.pallas import tpu as pltpu
from jax.sharding import PartitionSpec as P

HALF_ROOT = 0.5**0.5
GELU_C = (2.0 / 3.141592653589793) ** 0.5
CHUNK = 8


def kernel(
    n, m, levels,
    x_ref, og_ref, prm_ref, mix_ref,
    gi_ref, small_ref, gmix_ref,
    xin, pbuf, mixr, og_all, gzs, gzr, gz, lv, lg, gp, zsend, zall, gibuf, accm, sbuf,
    mix_sem, xs_send, xs_recv, p_send, p_recv,
    up_send, dn_send, xb_send, xa_send, og_recv,
    gz_send, gz_recv, z_send, z_recv, gi_send, gi_recv, sm_send, sm_recv,
):
    i = lax.axis_index("context")
    j = lax.axis_index("channel")
    channels, length = x_ref.shape
    width = channels // n
    rows = width * m
    tokens = n * length
    lines = n // 2
    zi, xi = i // 2, i % 2
    mine = i * rows + j * width
    home = mine // channels
    slot = (mine % channels) // width
    here = home == j
    scale = float(tokens) ** (-0.5)

    def owner(b):
        g = j * channels + b * width
        return g // rows, (g % rows) // width

    def dev(a, b):
        return {"context": a, "channel": b}

    def remote(src, dst, ssem, rsem, a, b):
        return pltpu.make_async_remote_copy(
            src_ref=src, dst_ref=dst, send_sem=ssem, recv_sem=rsem,
            device_id=dev(a, b), device_id_type=pl.DeviceIdType.MESH,
        )

    mix_copy = pltpu.make_async_copy(
        mix_ref.at[pl.ds(pl.multiple_of(i * rows, 16), rows), :], mixr, mix_sem
    )
    mix_copy.start()

    barrier = pltpu.get_barrier_semaphore()

    def hello(a, b):
        pl.semaphore_signal(
            barrier, inc=1, device_id=dev(a, b), device_id_type=pl.DeviceIdType.MESH
        )

    for b in range(n):
        oi, oj = owner(b)
        pl.when(jnp.logical_or(oi != i, oj != j))(functools.partial(hello, oi, oj))
        pl.when(jnp.logical_or(b != i, home != j))(functools.partial(hello, b, home))
    for off in range(1, m):
        hello(i, (j + off) % m)
    hello(zi * 2 + 1 - xi, j)
    pl.when(zi > 0)(functools.partial(hello, i - 2, j))
    pl.when(zi < lines - 1)(functools.partial(hello, i + 2, j))
    expected = (
        2 * n + m
        - 2 * here.astype(jnp.int32)
        + (zi > 0).astype(jnp.int32)
        + (zi < lines - 1).astype(jnp.int32)
    )
    pl.semaphore_wait(barrier, expected)

    def prm_copy(b, oi, oj):
        return remote(
            prm_ref.at[pl.ds(b * width, width), :], pbuf, p_send.at[b], p_recv, oi, oj
        )

    def x_copy(b, oi, oj):
        return remote(
            x_ref.at[pl.ds(b * width, width), :], xin.at[i], xs_send.at[b], xs_recv.at[i], oi, oj
        )

    for b in range(n):
        oi, oj = owner(b)
        away = jnp.logical_or(oi != i, oj != j)

        @pl.when(away)
        def _():
            @pl.when(oi == i)
            def _():
                prm_copy(b, oi, oj).start()

            x_copy(b, oi, oj).start()

        @pl.when(jnp.logical_not(away))
        def _():
            pbuf[...] = prm_ref[pl.ds(b * width, width), :]
            xin[i] = x_ref[pl.ds(b * width, width), :]

    def block_copy(src, q, ssem, target):
        return remote(src, og_all.at[q], ssem, og_recv.at[q], target, j)

    across = zi * 2 + 1 - xi

    def up(src, q, s):
        return block_copy(src, q, up_send.at[s], i + 2)

    def down(src, q, s):
        return block_copy(src, q, dn_send.at[s], i - 2)

    has_up = zi < lines - 1
    has_down = zi > 0

    @pl.when(has_up)
    def _():
        up(og_ref, i, 0).start()

    @pl.when(has_down)
    def _():
        down(og_ref, i, 0).start()

    block_copy(og_ref, i, xb_send.at[0], across).start()
    og_all[i] = og_ref[...]
    mix_copy.wait()

    def gz_copy(d, q):
        return remote(gzs.at[d, q], gzr.at[j, q], gz_send.at[d, q], gz_recv.at[j, q], i, d)

    def partial_gz(q):
        full = jnp.dot(mixr[...], og_all[q], preferred_element_type=jnp.float32)
        for d in range(m):
            piece = full[d * width : (d + 1) * width]

            @pl.when(d == j)
            def _():
                gz[:, pl.ds(pl.multiple_of(q * length, 128), length)] = piece

            @pl.when(d != j)
            def _():
                gzs[d, q] = piece.astype(jnp.bfloat16)
                gz_copy(d, q).start()

    partial_gz(i)

    for a in range(n):
        @pl.when(jnp.logical_or(a != i, home != j))
        def _():
            pltpu.make_async_remote_copy(
                src_ref=xin.at[a], dst_ref=xin.at[a], send_sem=xs_send.at[0], recv_sem=xs_recv.at[a],
                device_id=dev(a, home), device_id_type=pl.DeviceIdType.MESH,
            ).wait_recv()

        lv[0, :, a * length : (a + 1) * length] = xin[a].astype(jnp.float32)

    @pl.when(jnp.logical_not(here))
    def _():
        remote(pbuf, pbuf, p_send.at[0], p_recv, i, home).wait_recv()

    lane = lax.broadcasted_iota(jnp.int32, (CHUNK, tokens), 1)

    def later(value, d):
        if d % 128 == 0:
            return jnp.concatenate(
                [jnp.zeros((CHUNK, d), value.dtype), value[:, : tokens - d]], 1
            )
        return jnp.where(lane < d, 0.0, pltpu.roll(value, d, 1))

    def earlier(value, d):
        if d % 128 == 0:
            return jnp.concatenate([value[:, d:], jnp.zeros((CHUNK, d), value.dtype)], 1)
        return jnp.where(lane >= tokens - d, 0.0, pltpu.roll(value, tokens - d, 1))

    def forward_chunk(c, carry):
        at = pl.ds(pl.multiple_of(c * CHUNK, CHUNK), CHUNK)
        prm = pbuf[at, :]
        l0, l1 = HALF_ROOT * prm[:, 0:1], HALF_ROOT * prm[:, 1:2]
        h0, h1 = HALF_ROOT * prm[:, 2:3], HALF_ROOT * prm[:, 3:4]
        now = lv[0, at, :]
        mixed = jnp.zeros((CHUNK, tokens), jnp.float32)
        for k in range(levels):
            w = prm[:, 5 + k : 6 + k]
            if 2**k >= tokens:
                lagged = jnp.zeros_like(now)
            else:
                lagged = later(now, 2**k)
            lg[k, at, :] = lagged
            mixed = mixed + ((w * h0) * now + (w * h1) * lagged)
            now = (l0 * now + l1 * lagged).astype(jnp.bfloat16).astype(jnp.float32)
            lv[k + 1, at, :] = now
        mixed = mixed + prm[:, 4:5] * now
        square = mixed * mixed
        t = jnp.tanh(GELU_C * (mixed * (1.0 + 0.044715 * square)))
        half = 0.5 * (1.0 + t)
        gp[at, :] = half + 0.5 * mixed * (1.0 - t * t) * (GELU_C * (1.0 + 0.134145 * square))
        lv[levels + 1, at, :] = mixed * half
        return carry

    lax.fori_loop(0, width // CHUNK, forward_chunk, 0)
    zsend[...] = lv[levels + 1].astype(jnp.bfloat16)
    zall[j] = zsend[...]

    def z_copy(off):
        return remote(
            zsend, zall.at[j], z_send.at[off], z_recv.at[j], i, (j + off) % m
        )

    def og_wait(q):
        block_copy(og_all.at[q], q, xb_send.at[0], across).wait_recv()

    def step(s, carry):
        below, above = zi - s, zi + s

        @pl.when(below >= 0)
        def _():
            q = below * 2 + xi
            og_wait(q)

            @pl.when(has_up)
            def _():
                up(og_all.at[q], q, s).start()

            block_copy(og_all.at[q], q, xb_send.at[s], across).start()

        @pl.when(above < lines)
        def _():
            q = above * 2 + xi
            og_wait(q)

            @pl.when(has_down)
            def _():
                down(og_all.at[q], q, s).start()

            block_copy(og_all.at[q], q, xa_send.at[s], across).start()

        @pl.when(below >= 0)
        def _():
            partial_gz(below * 2 + xi)

        @pl.when(above < lines)
        def _():
            partial_gz(above * 2 + xi)

        back, forth = zi - s + 1, zi + s - 1

        @pl.when(back >= 0)
        def _():
            q = back * 2 + 1 - xi
            og_wait(q)
            partial_gz(q)

        @pl.when(jnp.logical_and(forth < lines, s > 1))
        def _():
            q = forth * 2 + 1 - xi
            og_wait(q)
            partial_gz(q)

        return carry

    lax.fori_loop(1, lines, step, 0)
    for last in (zi - lines + 1, zi + lines - 1):
        @pl.when(jnp.logical_and(last >= 0, last < lines))
        def _():
            q = last * 2 + 1 - xi
            og_wait(q)
            partial_gz(q)

    for off in range(1, m):
        z_copy(off).start()

    def collect(q, carry):
        at = pl.ds(pl.multiple_of(q * length, 128), length)
        total = gz[:, at]
        for d in range(m):
            @pl.when(d != j)
            def _():
                remote(
                    gzs.at[d, q], gzr.at[d, q], gz_send.at[d, q], gz_recv.at[d, q], i, d
                ).wait()
        for off in range(1, m):
            total = total + gzr[(j + off) % m, q].astype(jnp.float32)
        gz[:, at] = total
        return carry

    lax.fori_loop(0, n, collect, 0)

    lanes = lax.broadcasted_iota(jnp.int32, (CHUNK, accm.shape[1]), 1)

    def backward_chunk(c, carry):
        at = pl.ds(pl.multiple_of(c * CHUNK, CHUNK), CHUNK)
        prm = pbuf[at, :]
        l0, l1 = HALF_ROOT * prm[:, 0:1], HALF_ROOT * prm[:, 1:2]
        h0, h1 = HALF_ROOT * prm[:, 2:3], HALF_ROOT * prm[:, 3:4]
        gm = gz[at, :] * gp[at, :]

        def total(value):
            return jnp.sum(value, axis=1, keepdims=True)

        out = jnp.where(lanes == 4, total(gm * lv[levels, at, :]), 0.0)
        grad = prm[:, 4:5] * gm
        zero = jnp.zeros((CHUNK, 1), jnp.float32)
        low0, low1, high0, high1 = zero, zero, zero, zero
        for k in reversed(range(levels)):
            w = prm[:, 5 + k : 6 + k]
            now, lagged = lv[k, at, :], lg[k, at, :]
            a, b = total(now * gm), total(lagged * gm)
            low0, low1 = low0 + total(now * grad), low1 + total(lagged * grad)
            high0, high1 = high0 + w * a, high1 + w * b
            out = out + jnp.where(lanes == 5 + k, h0 * a + h1 * b, 0.0)
            direct = l0 * grad + (h0 * w) * gm
            if 2**k < tokens:
                back = l1 * grad + (h1 * w) * gm
                direct = direct + earlier(back, 2**k)
            grad = direct
        for position, value in enumerate((low0, low1, high0, high1)):
            out = out + jnp.where(lanes == position, HALF_ROOT * value, 0.0)
        accm[at, :] = out * scale
        gz[at, :] = grad
        return carry

    lax.fori_loop(0, width // CHUNK, backward_chunk, 0)

    place = pl.ds(pl.multiple_of(slot * width, 16), width)

    def gi_copy(a):
        return remote(
            gibuf.at[a], gi_ref.at[place, :], gi_send.at[a], gi_recv.at[slot], a, home
        )

    def sm_copy(a):
        return remote(sbuf, small_ref.at[slot], sm_send.at[a], sm_recv.at[slot], a, home)

    turned = accm[...].T
    sbuf[...] = turned[: sbuf.shape[0], :]
    for a in range(n):
        gibuf[a] = gz[:, a * length : (a + 1) * length].astype(jnp.bfloat16)
        away = jnp.logical_or(a != i, home != j)

        @pl.when(away)
        def _():
            gi_copy(a).start()
            sm_copy(a).start()

        @pl.when(jnp.logical_not(away))
        def _():
            gi_ref[place, :] = gibuf[a]
            small_ref[slot] = sbuf[...]

    for off in range(1, m):
        src = (j + off) % m
        remote(zsend, zall.at[src], z_send.at[off], z_recv.at[src], i, src).wait_recv()
    for d in range(m):
        total = jnp.zeros((width, channels), jnp.float32)
        for q in range(n):
            total = total + lax.dot_general(
                zall[d, :, q * length : (q + 1) * length], og_all[q],
                (((1,), (1,)), ((), ())), preferred_element_type=jnp.float32,
            )
        gmix_ref[d * width : (d + 1) * width, :] = total * scale

    for b in range(n):
        oi, oj = owner(b)

        @pl.when(jnp.logical_or(oi != i, oj != j))
        def _():
            @pl.when(oi == i)
            def _():
                prm_copy(b, oi, oj).wait_send()

            x_copy(b, oi, oj).wait_send()
            there = pl.ds(b * width, width)
            remote(gibuf.at[b], gi_ref.at[there, :], gi_send.at[b], gi_recv.at[b], oi, oj).wait_recv()
            remote(sbuf, small_ref.at[b], sm_send.at[b], sm_recv.at[b], oi, oj).wait_recv()

        @pl.when(jnp.logical_or(b != i, home != j))
        def _():
            gi_copy(b).wait_send()
            sm_copy(b).wait_send()

    for off in range(1, m):
        z_copy(off).wait_send()

    def sent(s, carry):
        @pl.when(jnp.logical_and(zi - s >= 0, has_up))
        def _():
            up(og_ref, i, s).wait_send()

        @pl.when(jnp.logical_and(zi + s < lines, has_down))
        def _():
            down(og_ref, i, s).wait_send()

        @pl.when(zi - s >= 0)
        def _():
            block_copy(og_ref, i, xb_send.at[s], across).wait_send()

        @pl.when(jnp.logical_and(zi + s < lines, s > 0))
        def _():
            block_copy(og_ref, i, xa_send.at[s], across).wait_send()

        return carry

    lax.fori_loop(0, lines, sent, 0)


def solution(mesh):
    n, m = mesh.shape["context"], mesh.shape["channel"]

    def shards(inputs, out_grad, low_pass, high_pass, level_weight, mix):
        channels, length = inputs.shape
        levels = level_weight.shape[0] - 1
        width = channels // n
        rows, tokens, lines = width * m, n * length, n // 2
        count = 4 + levels + 1
        tall = -(-count // 8) * 8
        wide = -(-count // 128) * 128
        prm = jnp.concatenate([low_pass, high_pass, level_weight], 0).T
        prm = jnp.pad(prm, ((0, 0), (0, wide - count)))
        vmem = pl.BlockSpec(memory_space=pltpu.VMEM)
        f32, bf16 = jnp.float32, jnp.bfloat16
        sem = pltpu.SemaphoreType.DMA
        padded = -(-width // 128) * 128
        gi, small, gmix = pl.pallas_call(
            functools.partial(kernel, n, m, levels),
            out_shape=(
                jax.ShapeDtypeStruct((channels, length), bf16),
                jax.ShapeDtypeStruct((n, tall, padded), f32),
                jax.ShapeDtypeStruct((rows, channels), f32),
            ),
            in_specs=[vmem, vmem, vmem, pl.BlockSpec(memory_space=pl.ANY)],
            out_specs=(vmem, vmem, vmem),
            scratch_shapes=[
                pltpu.VMEM((n, width, length), bf16),
                pltpu.VMEM((width, wide), f32),
                pltpu.VMEM((rows, channels), bf16),
                pltpu.VMEM((n, channels, length), bf16),
                pltpu.VMEM((m, n, width, length), bf16),
                pltpu.VMEM((m, n, width, length), bf16),
                pltpu.VMEM((width, tokens), f32),
                pltpu.VMEM((levels + 2, width, tokens), f32),
                pltpu.VMEM((levels, width, tokens), f32),
                pltpu.VMEM((width, tokens), f32),
                pltpu.VMEM((width, tokens), bf16),
                pltpu.VMEM((m, width, tokens), bf16),
                pltpu.VMEM((n, width, length), bf16),
                pltpu.VMEM((padded, wide), f32),
                pltpu.VMEM((tall, padded), f32),
                sem, sem((n,)), sem((n,)), sem((n,)), sem,
                sem((lines,)), sem((lines,)), sem((lines,)), sem((lines,)), sem((n,)),
                sem((m, n)), sem((m, n)), sem((m,)), sem((m,)),
                sem((n,)), sem((n,)), sem((n,)), sem((n,)),
            ],
            compiler_params=pltpu.CompilerParams(collective_id=0, has_side_effects=True),
        )(inputs, out_grad, prm, mix)
        table = small[:, :count, :width].transpose(1, 0, 2).reshape(count, channels)
        return gi, table[0:2], table[2:4], table[4:], gmix

    return jax.shard_map(
        shards,
        mesh=mesh,
        in_specs=(
            P("channel", "context"),
            P("channel", "context"),
            P(None, "channel"),
            P(None, "channel"),
            P(None, "channel"),
            P(None, "channel"),
        ),
        out_specs=(
            P("channel", "context"),
            P(None, "channel"),
            P(None, "channel"),
            P(None, "channel"),
            P("context", "channel"),
        ),
        check_vma=False,
    )
```

time: 236 us -> 79.7 us (0.34)
  waiting for transfers between devices: 108 us -> 0 us
  Pallas kernels: 0 us -> 70.6 us
  other arithmetic: 37.4 us -> 0.79 us
  blocking collectives: 34.1 us -> 0 us
  starting transfers between devices: 27.9 us -> 0 us
  between operations: 14.4 us -> 0.67 us
  matrix products: 6.95 us -> 0 us
    ppermute x9 -> x0, waiting for transfers between devices: 108 us -> none  [passed_along(): lax.ppermute(value, axis, [(source, source + steps) for source in range(l...]
    pallas_call x0 -> x1, Pallas kernels: none -> 70.6 us  [shards(): pl.pallas_call(functools.partial(kernel, n, m, levels), out_shape=(jax.Sh...]
    psum x1 -> x0, blocking collectives: 34.1 us -> none  [record(): found = lax.psum(found, 'context')]
    ppermute x9 -> x0, starting transfers between devices: 27.8 us -> none  [passed_along(): lax.ppermute(value, axis, [(source, source + steps) for source in range(l...]
    reduce_sum x11 -> x0, other arithmetic: 14.2 us -> none  [the longest x7 4.82 us: terms_of(): jnp.sum(present_wide * grad_branch, 1)]
    mul x19 -> x0, other arithmetic: 11.5 us -> none  [the longest x11 7.13 us: split_grad(): HALF_ROOT * (low_taps[1] * grad_now + high_taps[1] * grad_branch)]
    convert_element_type x17 -> x0, other arithmetic: 9.57 us -> none  [the longest x8 4.31 us: advance(): present_wide = present.astype(jnp.float32)]
    dot_general x2 -> x0, matrix products: 6.95 us -> none  [the longest x1 3.93 us: shards(): lax.dot_general(lax.all_gather(z_out, 'channel', axis=0, tiled=True), out...]
  transfers between devices with their start and end apart: 12 -> 0, of which waited for: 9 -> 0; matrix products, arithmetic and copies ran while one was open for 18% -> 0% of each run, Pallas kernels for 0% -> 0%
where the time goes in v1:
time: 79.7 us; the launch traced here: 79.4 us
  Pallas kernels  70.6 us (89%)
  local copies, waits for them, and re-layouts  7.3 us (9%)
    pallas_call x1, Pallas kernels, shards(): pl.pallas_call(functools.partial(kernel, n, m, levels), out_shape=(jax.Sh...  70.6 us
    unnamed x2, local copies, waits for them, and re-layouts  3.54 us
    slice x8, local copies, waits for them, and re-layouts, shards(): return (gi, table[0:2], table[2:4], table[4:], gmix)  2.07 us

profile of v1, /device:TPU:0, one launch (start us, length us, event | category | flops | bytes accessed | tf_op | source)
XLA Modules:
  0.0 79.4 jit_solution(7432974749696888885)
XLA Ops:
  0.6 0.8 pad_maximum_fusion
  1.4 0.1 copy.20
  1.6 0.7 pad.4.prm_ref
  2.3 70.6 %shard_map.101 = (bf16[512,256]{1,0:T(8,128)(2,1)}, f32[8,16,128]{2,1,0:T(8,128)}, f32[256,512]{1,0:T(8,128)}) custom-call(bf16[512,256]{1,0:T(8,128)(2,1)} %x_ref.1, bf16[512,256]{1,0:T(8,128)(2,1)} %og_ref.1, f32[512,128]{1,0:T(8,128)} %pad.4.prm_ref, bf16[2048,512]{1,0:T(8,128)(2,1)} %mix_ref.1), custom_call_target="tpu_custom_call" | custom-call | tf_op jit(solution)/shard_map/pallas_call | solution.py:428
  72.9 0.8 %slice_bitcast_fusion = f32[16,8,64]{2,0,1:T(8,128)S(1)} fusion(f32[8,16,128]{2,1,0:T(8,128)} %get-tuple-element.9), kind=kLoop, calls=%fused_computation | loop fusion | bytes 65536 | tf_op jit(solution)/shard_map/transpose | solution.py:460
  73.8 0.7 slice.27
  74.5 0.7 slice.25
  75.2 0.7 slice.23
  75.8 1.7 %copy.26 = bf16[512,256]{1,0:T(8,128)(2,1)} copy(bf16[512,256]{1,0:T(8,128)(2,1)} %get-tuple-element.18) | data formatting | bytes 524288
  77.5 1.9 %copy.27 = f32[256,512]{1,0:T(8,128)} copy(f32[256,512]{1,0:T(8,128)} %get-tuple-element.22) | data formatting | bytes 1048576
  (5 shorter events, 0.0 us)

commit v2 on v1

--- a/solution.py
+++ b/solution.py
@@ -10,13 +10,17 @@
 HALF_ROOT = 0.5**0.5
 GELU_C = (2.0 / 3.141592653589793) ** 0.5
 CHUNK = 8
+SEND = 0
+RELAY = 0
+AHEAD = 2
+RELAY_EARLY = True
 
 
 def kernel(
     n, m, levels,
     x_ref, og_ref, prm_ref, mix_ref,
-    gi_ref, small_ref, gmix_ref,
-    xin, pbuf, mixr, og_all, gzs, gzr, gz, lv, lg, gp, zsend, zall, gibuf, accm, sbuf,
+    gi_ref, table_ref, gmix_ref,
+    small, stage, xr_send, st_recv, xin, pbuf, mixr, og_all, gzs, gzr, gz, lv, lg, gp, zsend, zall, gibuf, accm, sbuf,
     mix_sem, xs_send, xs_recv, p_send, p_recv,
     up_send, dn_send, xb_send, xa_send, og_recv,
     gz_send, gz_recv, z_send, z_recv, gi_send, gi_recv, sm_send, sm_recv,
@@ -35,9 +39,17 @@
     here = home == j
     scale = float(tokens) ** (-0.5)
 
+    xor1, xor2 = j + 1 - 2 * (j % 2), (j + 2) % m
+    side = j // 2
+    near = home // 2 == side
+    sender = jnp.where(near, home, (home + 2) % m)
+
+    def owner_of(shard, b):
+        g = shard * channels + b * width
+        return g // rows, (g % rows) // width
+
     def owner(b):
-        g = j * channels + b * width
-        return g // rows, (g % rows) // width
+        return owner_of(j, b)
 
     def dev(a, b):
         return {"context": a, "channel": b}
@@ -60,21 +72,23 @@
             barrier, inc=1, device_id=dev(a, b), device_id_type=pl.DeviceIdType.MESH
         )
 
-    for b in range(n):
-        oi, oj = owner(b)
-        pl.when(jnp.logical_or(oi != i, oj != j))(functools.partial(hello, oi, oj))
-        pl.when(jnp.logical_or(b != i, home != j))(functools.partial(hello, b, home))
+    expected = m
     for off in range(1, m):
         hello(i, (j + off) % m)
     hello(zi * 2 + 1 - xi, j)
-    pl.when(zi > 0)(functools.partial(hello, i - 2, j))
-    pl.when(zi < lines - 1)(functools.partial(hello, i + 2, j))
-    expected = (
-        2 * n + m
-        - 2 * here.astype(jnp.int32)
-        + (zi > 0).astype(jnp.int32)
-        + (zi < lines - 1).astype(jnp.int32)
-    )
+    greetings = [(zi > 0, i - 2, j), (zi < lines - 1, i + 2, j)]
+    for b in range(n):
+        oi, oj = owner(b)
+        greetings.append((jnp.logical_or(oi != i, oj != j), oi, oj))
+        greetings.append((jnp.logical_or(b != i, home != j), b, home))
+        oi, oj = owner_of(xor2, b)
+        away = jnp.logical_or(oi != i, oj != j)
+        greetings.append((jnp.logical_and(oj // 2 == side, away), oi, oj))
+        away = jnp.logical_or(b != i, sender != j)
+        greetings.append((jnp.logical_and(jnp.logical_not(near), away), b, sender))
+    for wanted, a, b in greetings:
+        pl.when(wanted)(functools.partial(hello, a, b))
+        expected = expected + jnp.where(wanted, 1, 0)
     pl.semaphore_wait(barrier, expected)
 
     def prm_copy(b, oi, oj):
@@ -87,22 +101,53 @@
             x_ref.at[pl.ds(b * width, width), :], xin.at[i], xs_send.at[b], xs_recv.at[i], oi, oj
         )
 
-    for b in range(n):
-        oi, oj = owner(b)
-        away = jnp.logical_or(oi != i, oj != j)
-
-        @pl.when(away)
-        def _():
-            @pl.when(oi == i)
-            def _():
-                prm_copy(b, oi, oj).start()
-
-            x_copy(b, oi, oj).start()
-
-        @pl.when(jnp.logical_not(away))
-        def _():
-            pbuf[...] = prm_ref[pl.ds(b * width, width), :]
-            xin[i] = x_ref[pl.ds(b * width, width), :]
+    def stage_copy(b):
+        return remote(
+            x_ref.at[pl.ds(b * width, width), :], stage.at[b], xs_send.at[b], st_recv.at[b], i, xor2
+        )
+
+    def relay_copy(b, oi, oj):
+        return remote(stage.at[b], xin.at[i], xr_send.at[b], xs_recv.at[i], oi, oj)
+
+    def relay_inputs():
+        for b in range(n):
+            oi, oj = owner_of(xor2, b)
+
+            @pl.when(oj // 2 == side)
+            def _():
+                stage_copy(b).wait_recv()
+
+                @pl.when(jnp.logical_or(oi != i, oj != j))
+                def _():
+                    relay_copy(b, oi, oj).start()
+
+                @pl.when(jnp.logical_and(oi == i, oj == j))
+                def _():
+                    xin[i] = stage[b]
+
+    def send_inputs():
+        for b in range(n):
+            oi, oj = owner(b)
+            away = jnp.logical_or(oi != i, oj != j)
+
+            @pl.when(away)
+            def _():
+                @pl.when(oi == i)
+                def _():
+                    prm_copy(b, oi, oj).start()
+
+                @pl.when(oj // 2 == side)
+                def _():
+                    x_copy(b, oi, oj).start()
+
+                @pl.when(oj // 2 != side)
+                def _():
+                    stage_copy(b).start()
+
+            @pl.when(jnp.logical_not(away))
+            def _():
+                pbuf[...] = prm_ref[pl.ds(b * width, width), :]
+                xin[i] = x_ref[pl.ds(b * width, width), :]
 
     def block_copy(src, q, ssem, target):
         return remote(src, og_all.at[q], ssem, og_recv.at[q], target, j)
@@ -146,22 +191,6 @@
             def _():
                 gzs[d, q] = piece.astype(jnp.bfloat16)
                 gz_copy(d, q).start()
-
-    partial_gz(i)
-
-    for a in range(n):
-        @pl.when(jnp.logical_or(a != i, home != j))
-        def _():
-            pltpu.make_async_remote_copy(
-                src_ref=xin.at[a], dst_ref=xin.at[a], send_sem=xs_send.at[0], recv_sem=xs_recv.at[a],
-                device_id=dev(a, home), device_id_type=pl.DeviceIdType.MESH,
-            ).wait_recv()
-
-        lv[0, :, a * length : (a + 1) * length] = xin[a].astype(jnp.float32)
-
-    @pl.when(jnp.logical_not(here))
-    def _():
-        remote(pbuf, pbuf, p_send.at[0], p_recv, i, home).wait_recv()
 
     lane = lax.broadcasted_iota(jnp.int32, (CHUNK, tokens), 1)
 
@@ -202,14 +231,45 @@
         lv[levels + 1, at, :] = mixed * half
         return carry
 
-    lax.fori_loop(0, width // CHUNK, forward_chunk, 0)
-    zsend[...] = lv[levels + 1].astype(jnp.bfloat16)
-    zall[j] = zsend[...]
-
-    def z_copy(off):
-        return remote(
-            zsend, zall.at[j], z_send.at[off], z_recv.at[j], i, (j + off) % m
-        )
+    def z_copy(src, who, k, target):
+        return remote(src, zall.at[who], z_send.at[k], z_recv.at[who], i, target)
+
+    def z_start():
+        z_copy(zsend, j, 0, xor1).start()
+        z_copy(zsend, j, 1, xor2).start()
+
+    def z_relay():
+        z_copy(zsend, xor2, 1, xor2).wait_recv()
+        z_copy(zall.at[xor2], xor2, 2, xor1).start()
+
+    def z_arrive():
+        z_copy(zsend, xor1, 0, xor1).wait_recv()
+        z_copy(zsend, (xor1 + 2) % m, 2, xor1).wait_recv()
+
+    def z_finish():
+        z_copy(zsend, j, 0, xor1).wait_send()
+        z_copy(zsend, j, 1, xor2).wait_send()
+        z_copy(zsend, j, 2, xor1).wait_send()
+
+    def forward():
+        for a in range(n):
+            @pl.when(jnp.logical_or(a != i, sender != j))
+            def _():
+                pltpu.make_async_remote_copy(
+                    src_ref=xin.at[a], dst_ref=xin.at[a], send_sem=xs_send.at[0], recv_sem=xs_recv.at[a],
+                    device_id=dev(a, sender), device_id_type=pl.DeviceIdType.MESH,
+                ).wait_recv()
+
+            lv[0, :, a * length : (a + 1) * length] = xin[a].astype(jnp.float32)
+
+        @pl.when(jnp.logical_not(here))
+        def _():
+            remote(pbuf, pbuf, p_send.at[0], p_recv, i, home).wait_recv()
+
+        lax.fori_loop(0, width // CHUNK, forward_chunk, 0)
+        zsend[...] = lv[levels + 1].astype(jnp.bfloat16)
+        zall[j] = zsend[...]
+        z_start()
 
     def og_wait(q):
         block_copy(og_all.at[q], q, xb_send.at[0], across).wait_recv()
@@ -263,7 +323,26 @@
 
         return carry
 
-    lax.fori_loop(1, lines, step, 0)
+    def steps(first, last):
+        if last > first:
+            lax.fori_loop(first, last, step, 0)
+
+    if SEND == 0:
+        send_inputs()
+    partial_gz(i)
+    if RELAY == 0:
+        relay_inputs()
+    if AHEAD == 0:
+        forward()
+    marks = sorted({1, min(SEND, lines - 1) + 1, min(AHEAD, lines - 1) + 1, min(RELAY, lines - 1) + 1, lines})
+    for first, last in zip(marks[:-1], marks[1:]):
+        steps(first, last)
+        if last - 1 == min(SEND, lines - 1) and SEND > 0:
+            send_inputs()
+        if last - 1 == min(RELAY, lines - 1) and RELAY > 0:
+            relay_inputs()
+        if last - 1 == min(AHEAD, lines - 1) and AHEAD > 0:
+            forward()
     for last in (zi - lines + 1, zi + lines - 1):
         @pl.when(jnp.logical_and(last >= 0, last < lines))
         def _():
@@ -271,9 +350,8 @@
             og_wait(q)
             partial_gz(q)
 
-    for off in range(1, m):
-        z_copy(off).start()
-
+    if RELAY_EARLY:
+        z_relay()
     def collect(q, carry):
         at = pl.ds(pl.multiple_of(q * length, 128), length)
         total = gz[:, at]
@@ -299,27 +377,34 @@
         h0, h1 = HALF_ROOT * prm[:, 2:3], HALF_ROOT * prm[:, 3:4]
         gm = gz[at, :] * gp[at, :]
 
+        def fold(value):
+            while value.shape[1] % 256 == 0:
+                half = value.shape[1] // 2
+                value = value[:, :half] + value[:, half:]
+            parts = [value[:, p : p + 128] for p in range(0, value.shape[1], 128)]
+            return sum(parts[1:], parts[0])
+
         def total(value):
             return jnp.sum(value, axis=1, keepdims=True)
 
-        out = jnp.where(lanes == 4, total(gm * lv[levels, at, :]), 0.0)
+        out = jnp.where(lanes == 4, total(fold(gm * lv[levels, at, :])), 0.0)
         grad = prm[:, 4:5] * gm
-        zero = jnp.zeros((CHUNK, 1), jnp.float32)
+        zero = jnp.zeros((CHUNK, 128), jnp.float32)
         low0, low1, high0, high1 = zero, zero, zero, zero
         for k in reversed(range(levels)):
             w = prm[:, 5 + k : 6 + k]
             now, lagged = lv[k, at, :], lg[k, at, :]
-            a, b = total(now * gm), total(lagged * gm)
-            low0, low1 = low0 + total(now * grad), low1 + total(lagged * grad)
+            a, b = fold(now * gm), fold(lagged * gm)
+            low0, low1 = low0 + fold(now * grad), low1 + fold(lagged * grad)
             high0, high1 = high0 + w * a, high1 + w * b
-            out = out + jnp.where(lanes == 5 + k, h0 * a + h1 * b, 0.0)
+            out = out + jnp.where(lanes == 5 + k, total(h0 * a + h1 * b), 0.0)
             direct = l0 * grad + (h0 * w) * gm
             if 2**k < tokens:
                 back = l1 * grad + (h1 * w) * gm
                 direct = direct + earlier(back, 2**k)
             grad = direct
         for position, value in enumerate((low0, low1, high0, high1)):
-            out = out + jnp.where(lanes == position, HALF_ROOT * value, 0.0)
+            out = out + jnp.where(lanes == position, HALF_ROOT * total(value), 0.0)
         accm[at, :] = out * scale
         gz[at, :] = grad
         return carry
@@ -334,7 +419,7 @@
         )
 
     def sm_copy(a):
-        return remote(sbuf, small_ref.at[slot], sm_send.at[a], sm_recv.at[slot], a, home)
+        return remote(sbuf, small.at[slot], sm_send.at[a], sm_recv.at[slot], a, home)
 
     turned = accm[...].T
     sbuf[...] = turned[: sbuf.shape[0], :]
@@ -350,11 +435,11 @@
         @pl.when(jnp.logical_not(away))
         def _():
             gi_ref[place, :] = gibuf[a]
-            small_ref[slot] = sbuf[...]
-
-    for off in range(1, m):
-        src = (j + off) % m
-        remote(zsend, zall.at[src], z_send.at[off], z_recv.at[src], i, src).wait_recv()
+            small[slot] = sbuf[...]
+
+    if not RELAY_EARLY:
+        z_relay()
+    z_arrive()
     for d in range(m):
         total = jnp.zeros((width, channels), jnp.float32)
         for q in range(n):
@@ -376,15 +461,24 @@
             x_copy(b, oi, oj).wait_send()
             there = pl.ds(b * width, width)
             remote(gibuf.at[b], gi_ref.at[there, :], gi_send.at[b], gi_recv.at[b], oi, oj).wait_recv()
-            remote(sbuf, small_ref.at[b], sm_send.at[b], sm_recv.at[b], oi, oj).wait_recv()
+            remote(sbuf, small.at[b], sm_send.at[b], sm_recv.at[b], oi, oj).wait_recv()
+
+        ri, rj = owner_of(xor2, b)
+
+        @pl.when(jnp.logical_and(rj // 2 == side, jnp.logical_or(ri != i, rj != j)))
+        def _():
+            relay_copy(b, ri, rj).wait_send()
 
         @pl.when(jnp.logical_or(b != i, home != j))
         def _():
             gi_copy(b).wait_send()
             sm_copy(b).wait_send()
 
-    for off in range(1, m):
-        z_copy(off).wait_send()
+    for b in range(n):
+        part = pl.ds(b * width, width)
+        table_ref[:, part] = small[b, :, :width]
+
+    z_finish()
 
     def sent(s, carry):
         @pl.when(jnp.logical_and(zi - s >= 0, has_up))
@@ -425,16 +519,18 @@
         f32, bf16 = jnp.float32, jnp.bfloat16
         sem = pltpu.SemaphoreType.DMA
         padded = -(-width // 128) * 128
-        gi, small, gmix = pl.pallas_call(
+        gi, table, gmix = pl.pallas_call(
             functools.partial(kernel, n, m, levels),
             out_shape=(
                 jax.ShapeDtypeStruct((channels, length), bf16),
-                jax.ShapeDtypeStruct((n, tall, padded), f32),
+                jax.ShapeDtypeStruct((tall, channels), f32),
                 jax.ShapeDtypeStruct((rows, channels), f32),
             ),
             in_specs=[vmem, vmem, vmem, pl.BlockSpec(memory_space=pl.ANY)],
-            out_specs=(vmem, vmem, vmem),
+            out_specs=(vmem,) * 3,
             scratch_shapes=[
+                pltpu.VMEM((n, tall, padded), f32),
+                pltpu.VMEM((n, width, length), bf16), sem((n,)), sem((n,)),
                 pltpu.VMEM((n, width, length), bf16),
                 pltpu.VMEM((width, wide), f32),
                 pltpu.VMEM((rows, channels), bf16),
@@ -457,8 +553,7 @@
             ],
             compiler_params=pltpu.CompilerParams(collective_id=0, has_side_effects=True),
         )(inputs, out_grad, prm, mix)
-        table = small[:, :count, :width].transpose(1, 0, 2).reshape(count, channels)
-        return gi, table[0:2], table[2:4], table[4:], gmix
+        return gi, table[0:2], table[2:4], table[4:count], gmix
 
     return jax.shard_map(
         shards,

time: 79.7 us -> 70 us (0.88)
  the two profiles are of different devices: /device:TPU:0 before, /device:TPU:14 now
where the time goes in v2:
time: 70 us; the launch traced here: 69.6 us
  Pallas kernels  61 us (87%)
  local copies, waits for them, and re-layouts  7.16 us (10%)
  other arithmetic  0.79 us (1%)
    pallas_call x1, Pallas kernels, shards(): pl.pallas_call(functools.partial(kernel, n, m, levels), out_shape=(jax.Sh...  61 us
    unnamed x2, local copies, waits for them, and re-layouts  3.54 us
    slice x2, local copies, waits for them, and re-layouts, shards(): return (gi, table[0:2], table[2:4], table[4:count], gmix)  2.77 us

profile of v2, /device:TPU:14, one launch (start us, length us, event | category | flops | bytes accessed | tf_op | source)
XLA Modules:
  0.0 69.6 jit_solution(221094028140390321)
XLA Ops:
  0.6 0.8 %pad_maximum_fusion = f32[16,512]{1,0:T(8,128)S(1)} fusion(f32[12,512]{1,0:T(8,128)} %param.10, f32[2,512]{1,0:T(2,128)} %param.9, f32[2,512]{1,0:T(2,128)} %param.8), kind=kLoop, calls=%fused_computation | loop fusion | flops 16384 | bytes 65536 | tf_op jit(solution)/shard_map/concatenate | solution.py:516
  1.4 0.1 copy.14
  1.6 0.7 %pad.4.prm_ref = f32[512,128]{1,0:T(8,128)} pad(f32[512,16]{1,0:T(8,128)S(1)} %bitcast.1, f32[]{:T(128)} %constant.2.clone.1), padding=0_0x0_112 | pad | bytes 294916 | tf_op jit(solution)/shard_map/jit(_pad)/pad | solution.py:517
  2.3 61.0 %shard_map.101 = (bf16[512,256]{1,0:T(8,128)(2,1)}, f32[16,512]{1,0:T(8,128)}, f32[256,512]{1,0:T(8,128)}) custom-call(bf16[512,256]{1,0:T(8,128)(2,1)} %x_ref.1, bf16[512,256]{1,0:T(8,128)(2,1)} %og_ref.1, f32[512,128]{1,0:T(8,128)} %pad.4.prm_ref, bf16[2048,512]{1,0:T(8,128)(2,1)} %mix_ref.1), custom_call_target="tpu_custom_call" | custom-call | tf_op jit(solution)/shard_map/pallas_call | solution.py:522
  63.3 1.4 %fusion = (f32[2,512]{1,0:T(2,128)}, f32[2,512]{1,0:T(2,128)}) fusion(f32[16,512]{1,0:T(8,128)} %get-tuple-element.9), kind=kLoop, calls=%fused_computation.1 | loop fusion | bytes 16384 | tf_op jit(solution)/shard_map/slice | solution.py:556
  64.7 1.4 %slice.11 = f32[12,512]{1,0:T(8,128)} slice(f32[16,512]{1,0:T(8,128)} %get-tuple-element.9), slice={[4:16], [0:512]} | slice | bytes 49152 | tf_op jit(solution)/shard_map/slice | solution.py:556
  66.0 1.7 %copy.17 = bf16[512,256]{1,0:T(8,128)(2,1)} copy(bf16[512,256]{1,0:T(8,128)(2,1)} %get-tuple-element.18) | data formatting | bytes 524288
  67.7 1.9 %copy.18 = f32[256,512]{1,0:T(8,128)} copy(f32[256,512]{1,0:T(8,128)} %get-tuple-element.22) | data formatting | bytes 1048576
